TPU v7x, 128 devices: a whole 4x4x4 slice. The times are simulated.
128 devices in a mesh: dp: 8 (over y, core), feat: 16 (over z, x).
Axes of the slice: x: 4, y: 4, z: 4, core: 2. Of those that a mesh axis runs over, the one named last changes fastest.
Arguments:
- features: bfloat16 [32768, 8192], P('dp', 'feat'), may hold values from -6 to 6
- fixed_coef: float32 [8192], P('feat'), may hold values from -0.0625 to 0.0625
- member_score: float32 [32768], P('dp'), may hold values from -6 to 6
- clicks: int32 [32768], P('dp'), may hold values 0 or 1
- member_features: bfloat16 [32768, 256], P(('dp', 'feat')), may hold values from -6 to 6
- member_coef: float32 [1024, 256], P(('dp', 'feat')), may hold values from -0.375 to 0.375
- block_slot: int32 [32768], P(('dp', 'feat')), may hold values from 0 to 65535, as said below
Outputs:
- fixed_grad: float32 [8192], P('feat')
- member_coef_new: float32 [1024, 256], P(('dp', 'feat'))
- total_score: float32 [32768], P(('dp', 'feat'))
Inputs may be any that keep to these rules, and one draw needn't show every extreme that they name: All block_slot values differ. block_slot // 512 is the device (index along dp+feat) that owns the impression's member, and block_slot // 64 is the member. Every owner receives exactly 256 impressions. One device sends at most 6 of its impressions to one owner, and every device sends exactly 6 to some owner.
All inputs are finite; a program needn't handle non-finite values. Where the computation divides by a largest or mean magnitude, that divisor is 1e-20 or more. No bound on the sum of `clicks` on one device may be relied on, other than what follows from the above.
Results may differ from a plain program's by a relative error of at most 0.0093.
Values may be sent and summed in bfloat16 or wider, within the bound.
A program may use at most 64 MiB of HBM per device.

v0:
```python
import math
import jax
import jax.numpy as jnp
from jax import lax
from jax.sharding import PartitionSpec as P

BLK = 64
NEWTON = 3
ridge_weight = 1.0
high = lax.Precision.HIGHEST
inverse_sweeps = 20


def apply_inverse(system, vector):
    identity = jnp.eye(system.shape[1], dtype=system.dtype)
    bound = jnp.max(jnp.sum(jnp.abs(system), axis=2), axis=1)
    start = (2.0 / (1.0 + bound))[:, None, None] * identity[None, :, :]

    def sweep(index, approx):
        product = jnp.einsum("mbc,mcd->mbd", system, approx, precision=high)
        return 2.0 * approx - jnp.einsum("mbc,mcd->mbd", approx, product, precision=high)

    approx = lax.fori_loop(0, inverse_sweeps, sweep, start)
    return jnp.einsum("mbc,mc->mb", approx, vector, precision=high)


def newton_blocks(padded_rows, offset, label_pad, live_pad, coeffs):
    gram_matrix = jnp.einsum("mbk,mck->mbc", padded_rows, padded_rows, precision=high)
    identity = jnp.eye(padded_rows.shape[1], dtype=padded_rows.dtype)
    for iteration in range(NEWTON):
        linear = offset + jnp.einsum("mbk,mk->mb", padded_rows, coeffs, precision=high)
        probability = jax.nn.sigmoid(linear)
        gradient = (
            jnp.einsum(
                "mbk,mb->mk", padded_rows, live_pad * (probability - label_pad), precision=high
            )
            + ridge_weight * coeffs
        )
        weight_root = jnp.sqrt(live_pad * probability * (1.0 - probability))
        system = (
            ridge_weight * identity
            + weight_root[:, :, None] * gram_matrix * weight_root[:, None, :]
        )
        projected = weight_root * jnp.einsum("mbk,mk->mb", padded_rows, gradient, precision=high)
        solved = apply_inverse(system, projected)
        back_term = jnp.einsum("mbk,mb->mk", padded_rows, weight_root * solved, precision=high)
        coeffs = coeffs - (gradient - back_term) / ridge_weight
    return coeffs


def per_device(
    features, fixed_coef, member_score, clicks, member_features, member_coef, block_slot
):
    n_dp = lax.axis_size("dp")
    n_feat = lax.axis_size("feat")
    devices = n_dp * n_feat
    rows_own = member_features.shape[0]
    width = member_features.shape[1]
    slot_count = 2 * rows_own
    blocks = slot_count // BLK
    capacity = 3 * ((rows_own + devices - 1) // devices)
    row_start = lax.axis_index("feat") * rows_own
    coef_half = fixed_coef.astype(jnp.bfloat16)
    partial_score = jnp.dot(features, coef_half, preferred_element_type=jnp.float32)
    own_clicks = lax.dynamic_slice_in_dim(clicks, row_start, rows_own).astype(jnp.float32)
    fixed_score = lax.psum(partial_score, "feat")
    residual = (jax.nn.sigmoid(fixed_score + member_score) - clicks.astype(jnp.float32)).astype(
        jnp.bfloat16
    )
    own_score = lax.dynamic_slice_in_dim(fixed_score, row_start, rows_own)
    grad_part = jnp.dot(residual, features, preferred_element_type=jnp.float32)
    fixed_grad = lax.psum(grad_part, "dp") / math.sqrt(rows_own * devices)
    owner_dev = block_slot // slot_count
    local_slot = block_slot - owner_dev * slot_count
    onehot = (owner_dev[:, None] == jnp.arange(devices, dtype=jnp.int32)[None, :]).astype(jnp.int32)
    row_rank = jnp.sum(jnp.cumsum(onehot, axis=0) * onehot, axis=1) - 1
    send_place = owner_dev * capacity + row_rank
    rows_out = (
        jnp.zeros((devices * capacity, width), jnp.bfloat16).at[send_place].set(member_features)
    )
    tag_value = (local_slot * 2).astype(jnp.float32) + own_clicks
    score_buffer = jnp.zeros((devices * capacity,), jnp.float32).at[send_place].set(own_score)
    tag_buffer = jnp.full((devices * capacity,), -1.0, jnp.float32).at[send_place].set(tag_value)
    meta_out = jnp.stack([score_buffer, tag_buffer])
    rows_in = lax.all_to_all(
        rows_out.reshape(devices, capacity, width),
        ("dp", "feat"),
        split_axis=0,
        concat_axis=0,
        tiled=True,
    )
    meta_in = lax.all_to_all(
        meta_out.reshape(2, devices, capacity),
        ("dp", "feat"),
        split_axis=1,
        concat_axis=1,
        tiled=True,
    )
    rows_in = rows_in.reshape(devices * capacity, width)
    meta_in = meta_in.reshape(2, devices * capacity)
    tags_in = meta_in[1]
    valid_slot = tags_in >= 0.0
    tag_int = jnp.where(valid_slot, tags_in, 0.0).astype(jnp.int32)
    label_in = (tag_int % 2).astype(jnp.float32)
    where_local = jnp.where(valid_slot, tag_int // 2, slot_count)
    padded_rows = (
        jnp.zeros((slot_count + 1, width), jnp.float32)
        .at[where_local]
        .set(rows_in.astype(jnp.float32))[:slot_count]
        .reshape(blocks, BLK, width)
    )
    offset = (
        jnp.zeros((slot_count + 1,), jnp.float32)
        .at[where_local]
        .set(meta_in[0])[:slot_count]
        .reshape(blocks, BLK)
    )
    label_pad = (
        jnp.zeros((slot_count + 1,), jnp.float32)
        .at[where_local]
        .set(label_in)[:slot_count]
        .reshape(blocks, BLK)
    )
    live_pad = (
        jnp.zeros((slot_count + 1,), jnp.float32)
        .at[where_local]
        .set(1.0)[:slot_count]
        .reshape(blocks, BLK)
    )
    coeffs = newton_blocks(padded_rows, offset, label_pad, live_pad, member_coef)
    member_value = jnp.einsum("mbk,mk->mb", padded_rows, coeffs, precision=high).reshape(slot_count)
    back_value = jnp.where(valid_slot, member_value[jnp.minimum(where_local, slot_count - 1)], 0.0)
    returned = lax.all_to_all(
        back_value.reshape(devices, capacity),
        ("dp", "feat"),
        split_axis=0,
        concat_axis=0,
        tiled=True,
    )
    returned = returned.reshape(devices * capacity)
    total_score = own_score + returned[send_place]
    return (fixed_grad, coeffs, total_score)


def solution(mesh):
    return jax.shard_map(
        per_device,
        mesh=mesh,
        in_specs=(
            P("dp", "feat"),
            P("feat"),
            P("dp"),
            P("dp"),
            P(("dp", "feat"), None),
            P(("dp", "feat"), None),
            P(("dp", "feat")),
        ),
        out_specs=(P("feat"), P(("dp", "feat"), None), P(("dp", "feat"))),
        check_vma=False,
    )
```

profile of v0, /device:TPU:1, one launch (start us, length us, event | category | flops | bytes accessed | tf_op | source)
XLA Modules:
  0.0 235.6 jit_solution(464150204069671483)
XLA Ops:
  0.7 0.8 convert_add_fusion
  2.1 0.7 convert_element_type.65
  2.8 3.4 %fusion.54 = f32[1,4096]{1,0:T(1,128)S(1)} fusion(bf16[4096,512]{1,0:T(8,128)(2,1)} %param.13, bf16[512,1]{0,1:T(2,128)(2,1)S(1)} %reshape.293), kind=kOutput, calls=%fused_computation.124 | convolution fusion | flops 4194304 | bytes 4211712 | tf_op jit(solution)/shard_map/dot_general | solution.py:64
  6.1 62.3 %psum.14 = f32[4096]{0:T(1024)S(1)} all-reduce(f32[4096]{0:T(1024)S(1)} %bitcast.212), channel_id=1, replica_groups=mesh['dp'=8,'feat'=16] {'feat'}, use_global_device_ids=true, to_apply=%region_0.0 | all-reduce | flops 4096 | bytes 32768 | tf_op jit(solution)/shard_map/psum | solution.py:66
  68.5 1.4 scatter_custom_fusion
  70.0 1.4 scatter_custom_fusion.1
  71.6 0.8 copy.54
  72.3 18.9 %all-to-all-start = ((f32[2,128,6]{2,0,1:T(2,128)}), f32[2,128,6]{2,0,1:T(2,128)S(1)}, u32[]{:S(2)}, u32[]{:S(2)}) async-start(f32[2,128,6]{2,0,1:T(2,128)} %copy.54), calls=%async_computation | async-start | bytes 262144 | tf_op jit(solution)/shard_map/all_to_all | solution.py:92
  91.3 2.8 %fusion.55 = f32[1,512]{1,0:T(1,128)S(1)} fusion(bf16[4096,1]{0,1:T(2,128)(2,1)S(1)} %reshape.295, bf16[4096,512]{1,0:T(8,128)(2,1)} %param.13), kind=kOutput, calls=%fused_computation.125 | convolution fusion | flops 4194304 | bytes 4204544 | tf_op jit(solution)/shard_map/dot_general | solution.py:71
  94.2 12.8 %psum.15 = f32[512]{0:T(512)S(1)} all-reduce(f32[512]{0:T(512)S(1)} %bitcast.239), channel_id=1, replica_groups=mesh['dp'=8,'feat'=16] {'dp'}, use_global_device_ids=true, to_apply=%region_1.0 | all-reduce | flops 512 | bytes 4096 | tf_op jit(solution)/shard_map/psum | solution.py:72
  107.0 0.6 broadcast_multiply_fusion.3
  107.6 2.0 scatter_custom_fusion.2
  109.6 0.9 reshape.209
  110.5 9.4 %all-to-all-start.1 = ((bf16[128,6,256]{2,1,0:T(8,128)(2,1)}), bf16[128,6,256]{2,1,0:T(8,128)(2,1)S(1)}, u32[]{:S(2)}, u32[]{:S(2)}) async-start(bf16[128,6,256]{2,1,0:T(8,128)(2,1)} %reshape.209), calls=%async_computation.1 | async-start | bytes 1048576 | tf_op jit(solution)/shard_map/all_to_all | solution.py:85
  120.5 3.4 %scatter_custom_fusion.6 = f32[513]{0:T(1024)S(1)} fusion(s32[768]{0:T(1024)S(1)} %get-tuple-element.94, f32[768]{0:T(1024)S(1)} %fusion.33, f32[]{:T(128)} %constant.51.clone.1), kind=kCustom, calls=%fused_computation.98 | custom fusion | bytes 2056 | tf_op jit(solution)/shard_map/scatter | solution.py:121
  124.1 3.4 %scatter_custom_fusion.5 = f32[513]{0:T(1024)S(1)} fusion(s32[768]{0:T(1024)S(1)} %get-tuple-element.94, f32[768]{0:T(1024)S(1)} %reshape.277, f32[]{:T(128)} %constant.51.clone.1), kind=kCustom, calls=%fused_computation.100 | custom fusion | bytes 2056 | tf_op jit(solution)/shard_map/scatter | solution.py:115
  127.6 3.6 %scatter_custom_fusion.4 = f32[513]{0:T(1024)S(1)} fusion(s32[768]{0:T(1024)S(1)} %get-tuple-element.94, f32[768]{0:T(1024)S(1)} %broadcast.285, f32[]{:T(128)} %constant.51.clone.1), kind=kCustom, calls=%fused_computation.102 | custom fusion | bytes 2056 | tf_op jit(solution)/shard_map/scatter | solution.py:127
  131.2 2.8 %all-to-all-done.1 = bf16[128,6,256]{2,1,0:T(8,128)(2,1)S(1)} async-done(((bf16[128,6,256]{2,1,0:T(8,128)(2,1)}), bf16[128,6,256]{2,1,0:T(8,128)(2,1)S(1)}, u32[]{:S(2)}, u32[]{:S(2)}) %all-to-all-start.1) | async-done | bytes 393248 | tf_op jit(solution)/shard_map/all_to_all | solution.py:85
  134.1 5.6 %scatter_custom_fusion.3 = f32[513,256]{1,0:T(8,128)S(1)} fusion(s32[768]{0:T(1024)S(1)} %get-tuple-element.94, f32[768,256]{1,0:T(8,128)S(1)} %reshape.261, f32[]{:T(128)} %constant.51.clone.1), kind=kCustom, calls=%fused_computation.15 | custom fusion | bytes 525316 | tf_op jit(solution)/shard_map/scatter | solution.py:109
  139.8 0.6 fusion.27
  140.8 0.6 fusion.25
  141.4 0.6 abs_reduce_fusion.2
  142.4 20.0 %while.30 = (s32[]{:T(128)}, f32[8,64,64]{1,2,0:T(8,128)S(1)}, f32[8,64,64]{2,1,0:T(8,128)S(1)}, s32[]{:T(128)}) while((s32[]{:T(128)}, f32[8,64,64]{1,2,0:T(8,128)S(1)}, f32[8,64,64]{2,1,0:T(8,128)S(1)}, s32[]{:T(128)}) %tuple.70), condition=%wide.region_15.16_spmd, body=%wide.region_14.15_spmd.sunk | while | flops 50397184 | bytes 1048629 | solution.py:23
  142.4 0.5 fusion.130
  145.4 0.5 fusion.130
  146.4 0.5 fusion.130
  149.4 0.5 fusion.130
  150.4 0.5 fusion.130
  153.4 0.5 fusion.130
  154.4 0.5 fusion.130
  157.4 0.5 fusion.130
  158.4 0.5 fusion.130
  161.4 0.5 fusion.130
  163.1 0.6 fusion.23
  164.1 0.6 fusion.21
  165.2 20.0 %while.31 = (s32[]{:T(128)}, f32[8,64,64]{1,2,0:T(8,128)S(1)}, f32[8,64,64]{2,1,0:T(8,128)S(1)}, s32[]{:T(128)}) while((s32[]{:T(128)}, f32[8,64,64]{1,2,0:T(8,128)S(1)}, f32[8,64,64]{2,1,0:T(8,128)S(1)}, s32[]{:T(128)}) %tuple.73), condition=%wide.region_19.20_spmd, body=%wide.region_18.19_spmd.sunk | while | flops 50397184 | bytes 1048629 | solution.py:23
  165.3 0.5 fusion.136
  168.3 0.5 fusion.136
  169.3 0.5 fusion.136
  172.3 0.5 fusion.136
  173.3 0.5 fusion.136
  176.3 0.5 fusion.136
  177.3 0.5 fusion.136
  180.3 0.5 fusion.136
  181.3 0.5 fusion.136
  184.3 0.5 fusion.136
  186.0 0.5 fusion.19
  187.0 0.5 fusion.17
  188.1 20.0 %while.32 = (s32[]{:T(128)}, f32[8,64,64]{1,2,0:T(8,128)S(1)}, f32[8,64,64]{2,1,0:T(8,128)S(1)}, s32[]{:T(128)}) while((s32[]{:T(128)}, f32[8,64,64]{1,2,0:T(8,128)S(1)}, f32[8,64,64]{2,1,0:T(8,128)S(1)}, s32[]{:T(128)}) %tuple.76), condition=%wide.region_23.24_spmd, body=%wide.region_22.23_spmd.sunk | while | flops 50397184 | bytes 1048629 | solution.py:23
  190.2 0.5 fusion.142
  193.2 0.5 fusion.142
  194.2 0.5 fusion.142
  197.2 0.5 fusion.142
  198.2 0.5 fusion.142
  201.2 0.5 fusion.142
  202.2 0.5 fusion.142
  208.9 0.5 fusion.15
  209.5 5.0 %gather_fusion = f32[768]{0:T(1024)S(1)} fusion(f32[512]{0:T(512)S(1)} %reshape.214, s32[1024]{0:T(1024)S(1)} %pad_clamp_fusion.1), kind=kCustom, calls=%fused_computation | custom fusion | bytes 9216 | tf_op jit(solution)/shard_map/gather | solution.py:132
  214.7 0.6 bitcast_select_fusion.1
  215.3 7.0 %all-to-all-start.2 = ((f32[128,1,6]{2,1,0:T(1,128)}), f32[128,1,6]{2,1,0:T(1,128)S(1)}, u32[]{:S(2)}, u32[]{:S(2)}) async-start(f32[128,1,6]{2,1,0:T(1,128)} %bitcast.62), calls=%async_computation.2 | async-start | bytes 131072 | tf_op jit(solution)/shard_map/all_to_all | solution.py:133
  222.3 9.8 %all-to-all-done.2 = f32[128,1,6]{2,1,0:T(1,128)S(1)} async-done(((f32[128,1,6]{2,1,0:T(1,128)}), f32[128,1,6]{2,1,0:T(1,128)S(1)}, u32[]{:S(2)}, u32[]{:S(2)}) %all-to-all-start.2) | async-done | bytes 3104 | tf_op jit(solution)/shard_map/all_to_all | solution.py:133
  232.6 0.8 reduce.11
  233.6 1.4 gather_fusion.1
  234.9 0.6 dynamic-slice_add_fusion
  (239 shorter events, 50.8 us)
Async XLA Ops:
  0.6 90.6 %copy-start.2 = (s32[4096]{0:T(1024)S(1)}, s32[4096]{0:T(1024)}, u32[]{:S(2)}) copy-start(s32[4096]{0:T(1024)} %param.16) | copy-start | bytes 49156
  0.6 90.6 %copy-start.3 = (f32[4096]{0:T(1024)S(1)}, f32[4096]{0:T(1024)}, u32[]{:S(2)}) copy-start(f32[4096]{0:T(1024)} %param.15) | copy-start | bytes 49156
  72.3 38.2 %all-to-all-start = ((f32[2,128,6]{2,0,1:T(2,128)}), f32[2,128,6]{2,0,1:T(2,128)S(1)}, u32[]{:S(2)}, u32[]{:S(2)}) async-start(f32[2,128,6]{2,0,1:T(2,128)} %copy.54), calls=%async_computation | async-start | bytes 262144 | tf_op jit(solution)/shard_map/all_to_all | solution.py:92
  91.3 48.4 %copy-start = (f32[8,256]{1,0:T(8,128)S(1)}, f32[8,256]{1,0:T(8,128)}, u32[]{:S(2)}) copy-start(f32[8,256]{1,0:T(8,128)} %param.18) | copy-start | bytes 24580
  110.5 23.5 %all-to-all-start.1 = ((bf16[128,6,256]{2,1,0:T(8,128)(2,1)}), bf16[128,6,256]{2,1,0:T(8,128)(2,1)S(1)}, u32[]{:S(2)}, u32[]{:S(2)}) async-start(bf16[128,6,256]{2,1,0:T(8,128)(2,1)} %reshape.209), calls=%async_computation.1 | async-start | bytes 1048576 | tf_op jit(solution)/shard_map/all_to_all | solution.py:85
  208.9 26.7 %copy-start.1 = (f32[8,256]{1,0:T(8,128)}, f32[8,256]{1,0:T(8,128)S(1)}, u32[]{:S(2)}) copy-start(f32[8,256]{1,0:T(8,128)S(1)} %fusion.12) | copy-start | bytes 24580
  215.3 16.8 %all-to-all-start.2 = ((f32[128,1,6]{2,1,0:T(1,128)}), f32[128,1,6]{2,1,0:T(1,128)S(1)}, u32[]{:S(2)}, u32[]{:S(2)}) async-start(f32[128,1,6]{2,1,0:T(1,128)} %bitcast.62), calls=%async_computation.2 | async-start | bytes 131072 | tf_op jit(solution)/shard_map/all_to_all | solution.py:133
where the time goes:
time: 236 us
  blocking collectives  75.1 us (32%)
  matrix products  70.7 us (30%)
  starting transfers between devices  35.3 us (15%)
  local copies, waits for them, and re-layouts  32.6 us (14%)
  waiting for transfers between devices  12.6 us (5%)
  other arithmetic  5.86 us (2%)
    psum x1, blocking collectives, per_device(): fixed_score = lax.psum(partial_score, 'feat')  62.3 us
    dot_general x60, matrix products, sweep(): product = jnp.einsum('mbc,mcd->mbd', system, approx, precision=high)  32.8 us
    dot_general x60, matrix products, sweep(): jnp.einsum('mbc,mcd->mbd', approx, product, precision=high)  23.8 us
    all_to_all x1, starting transfers between devices, per_device(): lax.all_to_all(meta_out.reshape(2, devices, capacity), ('dp', 'feat'), sp...  18.9 us
    psum x1, blocking collectives, per_device(): fixed_grad = lax.psum(grad_part, 'dp') / math.sqrt(rows_own * devices)  12.8 us
    all_to_all x1, waiting for transfers between devices, per_device(): lax.all_to_all(back_value.reshape(devices, capacity), ('dp', 'feat'), spl...  9.8 us
    all_to_all x1, starting transfers between devices, per_device(): lax.all_to_all(rows_out.reshape(devices, capacity, width), ('dp', 'feat')...  9.4 us
    all_to_all x1, starting transfers between devices, per_device(): lax.all_to_all(back_value.reshape(devices, capacity), ('dp', 'feat'), spl...  6.99 us
  transfers between devices with their start and end apart: 3, of which 2 were waited for; matrix products, arithmetic and copies ran while one was open for 7% of the time, Pallas kernels for 0%

commit v1 on v0

--- a/solution.py
+++ b/solution.py
@@ -9,6 +9,12 @@
 ridge_weight = 1.0
 high = lax.Precision.HIGHEST
 inverse_sweeps = 20
+
+
+def gather_and_add(block, name):
+    parts = lax.all_gather(block, name, axis=0, tiled=False)
+    total = parts.sum(axis=0)
+    return total
 
 
 def apply_inverse(system, vector):
@@ -63,7 +69,7 @@
     coef_half = fixed_coef.astype(jnp.bfloat16)
     partial_score = jnp.dot(features, coef_half, preferred_element_type=jnp.float32)
     own_clicks = lax.dynamic_slice_in_dim(clicks, row_start, rows_own).astype(jnp.float32)
-    fixed_score = lax.psum(partial_score, "feat")
+    fixed_score = gather_and_add(partial_score, "feat")
     residual = (jax.nn.sigmoid(fixed_score + member_score) - clicks.astype(jnp.float32)).astype(
         jnp.bfloat16
     )

time: 236 us -> 189 us (0.80)
  blocking collectives: 75.1 us -> 33.5 us
  starting transfers between devices: 35.3 us -> 29.3 us
    psum x1 -> x0, blocking collectives: 62.3 us -> none  [per_device(): fixed_score = lax.psum(partial_score, 'feat')]
    all_gather x0 -> x1, blocking collectives: none -> 20.7 us  [gather_and_add(): parts = lax.all_gather(block, name, axis=0, tiled=False)]
    all_to_all x1, starting transfers between devices: 18.9 us -> 12.9 us  [per_device(): lax.all_to_all(meta_out.reshape(2, devices, capacity), ('dp', 'feat'), sp...]
  transfers between devices with their start and end apart: 3 -> 3, of which waited for: 2 -> 2; matrix products, arithmetic and copies ran while one was open for 7% -> 9% of each run, Pallas kernels for 0% -> 0%
where the time goes in v1:
time: 189 us; the launch traced here: 188 us
  matrix products  70.7 us (37%)
  blocking collectives  33.5 us (18%)
  local copies, waits for them, and re-layouts  32.7 us (17%)
  starting transfers between devices  29.3 us (16%)
  waiting for transfers between devices  12.6 us (7%)
  other arithmetic  5.87 us (3%)
  loops' own time  2.3 us (1%)
    dot_general x60, matrix products, sweep(): product = jnp.einsum('mbc,mcd->mbd', system, approx, precision=high)  32.8 us
    dot_general x60, matrix products, sweep(): jnp.einsum('mbc,mcd->mbd', approx, product, precision=high)  23.8 us
    all_gather x1, blocking collectives, gather_and_add(): parts = lax.all_gather(block, name, axis=0, tiled=False)  20.7 us
    all_to_all x1, starting transfers between devices, per_device(): lax.all_to_all(meta_out.reshape(2, devices, capacity), ('dp', 'feat'), sp...  12.9 us
    psum x1, blocking collectives, per_device(): fixed_grad = lax.psum(grad_part, 'dp') / math.sqrt(rows_own * devices)  12.8 us
    all_to_all x1, waiting for transfers between devices, per_device(): lax.all_to_all(back_value.reshape(devices, capacity), ('dp', 'feat'), spl...  9.8 us
    all_to_all x1, starting transfers between devices, per_device(): lax.all_to_all(rows_out.reshape(devices, capacity, width), ('dp', 'feat')...  9.4 us
    all_to_all x1, starting transfers between devices, per_device(): lax.all_to_all(back_value.reshape(devices, capacity), ('dp', 'feat'), spl...  6.99 us
  transfers between devices with their start and end apart: 3, of which 2 were waited for; matrix products, arithmetic and copies ran while one was open for 9% of the time, Pallas kernels for 0%

profile of v1, /device:TPU:1, one launch (start us, length us, event | category | flops | bytes accessed | tf_op | source)
XLA Modules:
  0.0 188.1 jit_solution(16374158221362843522)
XLA Ops:
  0.6 0.8 convert_add_fusion
  2.0 0.7 convert_element_type.65
  2.7 3.4 %fusion.54 = f32[1,4096]{1,0:T(1,128)S(1)} fusion(bf16[4096,512]{1,0:T(8,128)(2,1)} %param.13, bf16[512,1]{0,1:T(2,128)(2,1)S(1)} %reshape.294), kind=kOutput, calls=%fused_computation.124 | convolution fusion | flops 4194304 | bytes 4211712 | tf_op jit(solution)/shard_map/dot_general | solution.py:70
  6.1 20.7 %all-gather = f32[65536]{0:T(1024)S(1)} all-gather(f32[4096]{0:T(1024)S(1)} %bitcast.212), channel_id=2, replica_groups=mesh['dp'=8,'feat'=16] {'feat'}, dimensions={0}, use_global_device_ids=true | all-gather | bytes 278528 | tf_op jit(solution)/shard_map/all_gather | solution.py:15
  27.0 1.4 scatter_custom_fusion
  28.5 1.4 scatter_custom_fusion.1
  30.1 0.8 copy.54
  30.9 12.9 %all-to-all-start = ((f32[2,128,6]{2,0,1:T(2,128)}), f32[2,128,6]{2,0,1:T(2,128)S(1)}, u32[]{:S(2)}, u32[]{:S(2)}) async-start(f32[2,128,6]{2,0,1:T(2,128)} %copy.54), calls=%async_computation | async-start | bytes 262144 | tf_op jit(solution)/shard_map/all_to_all | solution.py:98
  43.9 2.8 %fusion.55 = f32[1,512]{1,0:T(1,128)S(1)} fusion(bf16[4096,1]{0,1:T(2,128)(2,1)S(1)} %reshape.296, bf16[4096,512]{1,0:T(8,128)(2,1)} %param.13), kind=kOutput, calls=%fused_computation.125 | convolution fusion | flops 4194304 | bytes 4204544 | tf_op jit(solution)/shard_map/dot_general | solution.py:77
  46.7 12.8 %psum.7 = f32[512]{0:T(512)S(1)} all-reduce(f32[512]{0:T(512)S(1)} %bitcast.239), channel_id=1, replica_groups=mesh['dp'=8,'feat'=16] {'dp'}, use_global_device_ids=true, to_apply=%region_1.0 | all-reduce | flops 512 | bytes 4096 | tf_op jit(solution)/shard_map/psum | solution.py:78
  59.5 0.6 broadcast_multiply_fusion.3
  60.1 2.0 %scatter_custom_fusion.2 = bf16[768,256]{1,0:T(8,128)(2,1)S(1)} fusion(s32[256]{0:T(256)S(1)} %compare_select_fusion.8, bf16[256,256]{1,0:T(8,128)(2,1)} %param.17, bf16[]{:T(256)} %constant.104.clone.1), kind=kCustom, calls=%fused_computation.24 | custom fusion | bytes 393728 | tf_op jit(solution)/shard_map/scatter | solution.py:85
  62.1 0.9 reshape.209
  63.0 9.4 %all-to-all-start.1 = ((bf16[128,6,256]{2,1,0:T(8,128)(2,1)}), bf16[128,6,256]{2,1,0:T(8,128)(2,1)S(1)}, u32[]{:S(2)}, u32[]{:S(2)}) async-start(bf16[128,6,256]{2,1,0:T(8,128)(2,1)} %reshape.209), calls=%async_computation.1 | async-start | bytes 1048576 | tf_op jit(solution)/shard_map/all_to_all | solution.py:91
  73.0 3.4 %scatter_custom_fusion.6 = f32[513]{0:T(1024)S(1)} fusion(s32[768]{0:T(1024)S(1)} %get-tuple-element.94, f32[768]{0:T(1024)S(1)} %fusion.33, f32[]{:T(128)} %constant.48.clone.1), kind=kCustom, calls=%fused_computation.98 | custom fusion | bytes 2056 | tf_op jit(solution)/shard_map/scatter | solution.py:127
  76.6 3.4 %scatter_custom_fusion.5 = f32[513]{0:T(1024)S(1)} fusion(s32[768]{0:T(1024)S(1)} %get-tuple-element.94, f32[768]{0:T(1024)S(1)} %reshape.277, f32[]{:T(128)} %constant.48.clone.1), kind=kCustom, calls=%fused_computation.100 | custom fusion | bytes 2056 | tf_op jit(solution)/shard_map/scatter | solution.py:121
  80.1 3.6 %scatter_custom_fusion.4 = f32[513]{0:T(1024)S(1)} fusion(s32[768]{0:T(1024)S(1)} %get-tuple-element.94, f32[768]{0:T(1024)S(1)} %broadcast.285, f32[]{:T(128)} %constant.48.clone.1), kind=kCustom, calls=%fused_computation.102 | custom fusion | bytes 2056 | tf_op jit(solution)/shard_map/scatter | solution.py:133
  83.7 2.8 %all-to-all-done.1 = bf16[128,6,256]{2,1,0:T(8,128)(2,1)S(1)} async-done(((bf16[128,6,256]{2,1,0:T(8,128)(2,1)}), bf16[128,6,256]{2,1,0:T(8,128)(2,1)S(1)}, u32[]{:S(2)}, u32[]{:S(2)}) %all-to-all-start.1) | async-done | bytes 393248 | tf_op jit(solution)/shard_map/all_to_all | solution.py:91
  86.6 5.6 %scatter_custom_fusion.3 = f32[513,256]{1,0:T(8,128)S(1)} fusion(s32[768]{0:T(1024)S(1)} %get-tuple-element.94, f32[768,256]{1,0:T(8,128)S(1)} %reshape.261, f32[]{:T(128)} %constant.48.clone.1), kind=kCustom, calls=%fused_computation.15 | custom fusion | bytes 525316 | tf_op jit(solution)/shard_map/scatter | solution.py:115
  92.3 0.6 fusion.27
  93.3 0.6 fusion.25
  93.9 0.6 abs_reduce_fusion.2
  94.9 20.0 %while.30 = (s32[]{:T(128)}, f32[8,64,64]{1,2,0:T(8,128)S(1)}, f32[8,64,64]{2,1,0:T(8,128)S(1)}, s32[]{:T(128)}) while((s32[]{:T(128)}, f32[8,64,64]{1,2,0:T(8,128)S(1)}, f32[8,64,64]{2,1,0:T(8,128)S(1)}, s32[]{:T(128)}) %tuple.70), condition=%wide.region_15.16_spmd, body=%wide.region_14.15_spmd.sunk | while | flops 50397184 | bytes 1048629 | solution.py:29
  95.9 0.5 fusion.130
  98.9 0.5 fusion.130
  99.9 0.5 fusion.130
  102.9 0.5 fusion.130
  103.9 0.5 fusion.130
  106.9 0.5 fusion.130
  107.9 0.5 fusion.130
  110.9 0.5 fusion.130
  111.9 0.5 fusion.130
  115.7 0.6 fusion.23
  116.7 0.6 fusion.21
  117.8 20.0 %while.31 = (s32[]{:T(128)}, f32[8,64,64]{1,2,0:T(8,128)S(1)}, f32[8,64,64]{2,1,0:T(8,128)S(1)}, s32[]{:T(128)}) while((s32[]{:T(128)}, f32[8,64,64]{1,2,0:T(8,128)S(1)}, f32[8,64,64]{2,1,0:T(8,128)S(1)}, s32[]{:T(128)}) %tuple.73), condition=%wide.region_19.20_spmd, body=%wide.region_18.19_spmd.sunk | while | flops 50397184 | bytes 1048629 | solution.py:29
  117.8 0.5 fusion.136
  118.8 0.5 fusion.136
  121.8 0.5 fusion.136
  122.8 0.5 fusion.136
  125.8 0.5 fusion.136
  126.8 0.5 fusion.136
  129.8 0.5 fusion.136
  130.8 0.5 fusion.136
  133.8 0.5 fusion.136
  134.8 0.5 fusion.136
  138.5 0.5 fusion.19
  139.5 0.5 fusion.17
  140.6 20.0 %while.32 = (s32[]{:T(128)}, f32[8,64,64]{1,2,0:T(8,128)S(1)}, f32[8,64,64]{2,1,0:T(8,128)S(1)}, s32[]{:T(128)}) while((s32[]{:T(128)}, f32[8,64,64]{1,2,0:T(8,128)S(1)}, f32[8,64,64]{2,1,0:T(8,128)S(1)}, s32[]{:T(128)}) %tuple.76), condition=%wide.region_23.24_spmd, body=%wide.region_22.23_spmd.sunk | while | flops 50397184 | bytes 1048629 | solution.py:29
  143.7 0.5 fusion.142
  146.7 0.5 fusion.142
  147.7 0.5 fusion.142
  150.7 0.5 fusion.142
  151.7 0.5 fusion.142
  154.7 0.5 fusion.142
  155.7 0.5 fusion.142
  158.7 0.5 fusion.142
  161.4 0.5 fusion.15
  162.1 5.0 %gather_fusion = f32[768]{0:T(1024)S(1)} fusion(f32[512]{0:T(512)S(1)} %reshape.214, s32[1024]{0:T(1024)S(1)} %pad_clamp_fusion.1), kind=kCustom, calls=%fused_computation | custom fusion | bytes 9216 | tf_op jit(solution)/shard_map/gather | solution.py:138
  167.2 0.6 bitcast_select_fusion.1
  167.8 7.0 %all-to-all-start.2 = ((f32[128,1,6]{2,1,0:T(1,128)}), f32[128,1,6]{2,1,0:T(1,128)S(1)}, u32[]{:S(2)}, u32[]{:S(2)}) async-start(f32[128,1,6]{2,1,0:T(1,128)} %bitcast.62), calls=%async_computation.2 | async-start | bytes 131072 | tf_op jit(solution)/shard_map/all_to_all | solution.py:139
  174.9 9.8 %all-to-all-done.2 = f32[128,1,6]{2,1,0:T(1,128)S(1)} async-done(((f32[128,1,6]{2,1,0:T(1,128)}), f32[128,1,6]{2,1,0:T(1,128)S(1)}, u32[]{:S(2)}, u32[]{:S(2)}) %all-to-all-start.2) | async-done | bytes 3104 | tf_op jit(solution)/shard_map/all_to_all | solution.py:139
  185.2 0.8 reduce.11
  186.1 1.4 gather_fusion.1
  187.5 0.6 dynamic-slice_add_fusion
  (241 shorter events, 50.9 us)
Async XLA Ops:
  1.8 42.0 %copy-start.2 = (s32[4096]{0:T(1024)S(1)}, s32[4096]{0:T(1024)}, u32[]{:S(2)}) copy-start(s32[4096]{0:T(1024)} %param.16) | copy-start | bytes 49156
  1.8 42.0 %copy-start.3 = (f32[4096]{0:T(1024)S(1)}, f32[4096]{0:T(1024)}, u32[]{:S(2)}) copy-start(f32[4096]{0:T(1024)} %param.15) | copy-start | bytes 49156
  30.9 32.2 %all-to-all-start = ((f32[2,128,6]{2,0,1:T(2,128)}), f32[2,128,6]{2,0,1:T(2,128)S(1)}, u32[]{:S(2)}, u32[]{:S(2)}) async-start(f32[2,128,6]{2,0,1:T(2,128)} %copy.54), calls=%async_computation | async-start | bytes 262144 | tf_op jit(solution)/shard_map/all_to_all | solution.py:98
  43.9 48.4 %copy-start = (f32[8,256]{1,0:T(8,128)S(1)}, f32[8,256]{1,0:T(8,128)}, u32[]{:S(2)}) copy-start(f32[8,256]{1,0:T(8,128)} %param.18) | copy-start | bytes 24580
  63.0 23.5 %all-to-all-start.1 = ((bf16[128,6,256]{2,1,0:T(8,128)(2,1)}), bf16[128,6,256]{2,1,0:T(8,128)(2,1)S(1)}, u32[]{:S(2)}, u32[]{:S(2)}) async-start(bf16[128,6,256]{2,1,0:T(8,128)(2,1)} %reshape.209), calls=%async_computation.1 | async-start | bytes 1048576 | tf_op jit(solution)/shard_map/all_to_all | solution.py:91
  161.4 26.7 %copy-start.1 = (f32[8,256]{1,0:T(8,128)}, f32[8,256]{1,0:T(8,128)S(1)}, u32[]{:S(2)}) copy-start(f32[8,256]{1,0:T(8,128)S(1)} %fusion.12) | copy-start | bytes 24580
  167.8 16.8 %all-to-all-start.2 = ((f32[128,1,6]{2,1,0:T(1,128)}), f32[128,1,6]{2,1,0:T(1,128)S(1)}, u32[]{:S(2)}, u32[]{:S(2)}) async-start(f32[128,1,6]{2,1,0:T(1,128)} %bitcast.62), calls=%async_computation.2 | async-start | bytes 131072 | tf_op jit(solution)/shard_map/all_to_all | solution.py:139
